TPU v7x, 256 devices: a whole 4x4x8 slice. The times are simulated.
256 devices in a mesh: seq: 32 (over y_hi, z, core), mp: 8 (over y_lo, x).
Axes of the slice: x: 4, y: 4 (y_hi: 2, y_lo: 2; y = y_hi * 2 + y_lo), z: 8, core: 2. Of those that a mesh axis runs over, the one named last changes fastest.
Arguments:
- tokens: bfloat16 [8192, 4096], P('seq', 'mp'), may hold values from -16 to 16
- grad_out: bfloat16 [8192, 4096], P('seq', 'mp'), may hold values from -6 to 6
- w_query: bfloat16 [4096, 4096], P('seq', 'mp'), may hold values from -0.09375 to 0.09375
- w_key: bfloat16 [4096, 1024], P('seq', 'mp'), may hold values from -0.09375 to 0.09375
- w_value: bfloat16 [4096, 1024], P('seq', 'mp'), may hold values from -0.09375 to 0.09375
- doc_lengths: int32 [4], replicated, may hold values from 1 to 48, 64 in all
Outputs:
- grad_tokens: bfloat16 [8192, 4096], P('seq', 'mp')
- grad_w_query: float32 [4096, 4096], P('seq', 'mp')
- grad_w_key: float32 [4096, 1024], P('seq', 'mp')
- grad_w_value: float32 [4096, 1024], P('seq', 'mp')
Inputs may be any that keep to these rules, and one draw needn't show every extreme that they name: `doc_lengths`: the lengths sum to 64.
All inputs are finite; a program needn't handle non-finite values.
Results may differ from a plain program's by a relative error of at most 0.03.
The roundings to bfloat16 on the way count: a program that leaves them out, or rounds other values in their place, can miss the bound.
Values may be sent and summed in bfloat16 or wider, within the bound.
No kernel may reach another device: no remote copies, remote signals or barrier semaphores. Data moves between devices by JAX's collectives and lax.ppermute only.
A program may use at most 64 MiB of HBM per device.

v0:
```python
import jax
import jax.numpy as jnp
from jax import lax
from jax.sharding import PartitionSpec as P

HEAD_DIM = 128
WINDOW = 4096
ALIGN = 128
THETA = 10000.0
CONTRACT_LAST = (((1,), (1,)), ((), ()))
CONTRACT_FIRST = (((0,), (0,)), ((), ()))


def from_everyone(value, axis):
    peers = lax.axis_size(axis)
    return lax.all_to_all(
        jnp.broadcast_to(value[None], (peers, *value.shape)), axis, 0, 0, tiled=True
    )


def in_order(parts, dim):
    parts = jnp.moveaxis(parts, 0, dim)
    dims = parts.shape
    return parts.reshape(*dims[:dim], dims[dim] * dims[dim + 1], *dims[dim + 2 :])


def gather_directly(value, axis, dim):
    parts = from_everyone(value, axis)
    return in_order(parts, dim)


def shifted(value, axis, by):
    peers = lax.axis_size(axis)
    pairs = [(i, i + by) for i in range(peers) if 0 <= i + by < peers]
    return lax.ppermute(value, axis, pairs)


def split_up(value, dim, peers):
    dims = value.shape
    parts = value.reshape(*dims[:dim], peers, dims[dim] // peers, *dims[dim + 1 :])
    return jnp.moveaxis(parts, dim, 0)


def summed_on_arrival(value, axis, dim):
    peers = lax.axis_size(axis)
    parts = lax.all_to_all(split_up(value, dim, peers), axis, 0, 0, tiled=True)
    return jnp.sum(parts.astype(jnp.float32), axis=0)


def list_offsets(positions, ends, lengths):
    after = positions[:, None] >= ends[None, :]
    member = jnp.sum(after.astype(jnp.int32), axis=1)
    before = jnp.sum(jnp.where(after, lengths[None, :] * ALIGN, 0), axis=1)
    return (member, positions - before)


def rope_tables(offsets):
    half = HEAD_DIM // 2
    inverse = THETA ** (-(jnp.arange(half, dtype=jnp.float32) * 2.0 / HEAD_DIM))
    angle = offsets.astype(jnp.float32)[:, None] * inverse[None, :]
    angle = jnp.concatenate([angle, angle], axis=1)
    return (jnp.cos(angle), jnp.sin(angle))


def rotate(vectors, cosine, sine, direction):
    half = vectors.shape[-1] // 2
    turned = jnp.concatenate([-vectors[..., half:], vectors[..., :half]], axis=-1)
    return vectors * cosine[:, None, :] + direction * turned * sine[:, None, :]


def local(tokens, grad_out, w_query, w_key, w_value, doc_lengths):
    rows = tokens.shape[0]
    head_cols = w_query.shape[1]
    kv_cols = w_key.shape[1]
    heads_here = head_cols // HEAD_DIM
    kv_here = kv_cols // HEAD_DIM
    group = heads_here // kv_here
    span = WINDOW // rows
    block = min(512, WINDOW)
    count = WINDOW // block
    scale = HEAD_DIM ** (-0.5)
    first = lax.axis_index("seq") * rows
    ends = jnp.cumsum(doc_lengths) * ALIGN
    own_pos = first + jnp.arange(rows, dtype=jnp.int32)
    own_member, own_offset = list_offsets(own_pos, ends, doc_lengths)
    cosine, sine = rope_tables(own_offset)
    weights_all = jnp.concatenate([w_query, w_key, w_value], axis=1)
    whole = gather_directly(tokens, "mp", 1)
    panel = lax.all_gather(weights_all, "seq", axis=0, tiled=True)
    projected = jnp.dot(whole, panel, preferred_element_type=jnp.float32)
    query = rotate(projected[:, :head_cols].reshape(rows, heads_here, HEAD_DIM), cosine, sine, 1.0)
    query = query.astype(jnp.bfloat16).reshape(rows, kv_here, group, HEAD_DIM)
    keys = rotate(
        projected[:, head_cols : head_cols + kv_cols].reshape(rows, kv_here, HEAD_DIM),
        cosine,
        sine,
        1.0,
    ).astype(jnp.bfloat16)
    values = projected[:, head_cols + kv_cols :].astype(jnp.bfloat16)
    keys_flat = keys.reshape(rows, kv_cols)
    levels = (span - 1).bit_length()
    hops = [1] + [2**level for level in range(levels)]
    stack = (keys_flat[None], values[None])
    for number, hop in enumerate(hops):
        arrived = shifted((stack[0], stack[1]), "seq", hop)
        if number == 0:
            stack = arrived
        else:
            stack = (
                jnp.concatenate([arrived[0], stack[0]], axis=0),
                jnp.concatenate([arrived[1], stack[1]], axis=0),
            )
    window_keys, window_values = (stack[0], stack[1])
    window_keys = window_keys.reshape(count, block, kv_here, HEAD_DIM)
    window_values = window_values.reshape(count, block, kv_here, HEAD_DIM)
    window_pos = first - WINDOW + jnp.arange(WINDOW, dtype=jnp.int32)
    window_member, _ = list_offsets(window_pos, ends, doc_lengths)
    window_pos = window_pos.reshape(count, block)
    window_member = window_member.reshape(count, block)
    own_values = values.reshape(rows, kv_here, HEAD_DIM)

    def scores_for(key_block, key_pos, key_member):
        raw = (
            jnp.einsum("qagd,kad->agqk", query, key_block, preferred_element_type=jnp.float32)
            * scale
        )
        gap = own_pos[:, None] - key_pos[None, :]
        live = (
            (key_pos[None, :] >= 0)
            & (gap >= 0)
            & (gap < WINDOW)
            & (own_member[:, None] == key_member[None, :])
        )
        return jnp.where(live, raw, -jnp.inf)

    first_scores = scores_for(keys, own_pos, own_member)
    top = jnp.max(first_scores, axis=-1)
    mass = jnp.sum(jnp.exp(first_scores - top[..., None]), axis=-1)

    def absorb(carry, inputs):
        top, mass = carry
        key_block, key_pos, key_member = inputs
        scores = scores_for(key_block, key_pos, key_member)
        new_top = jnp.maximum(top, jnp.max(scores, axis=-1))
        factor = jnp.exp(top - new_top)
        mass = mass * factor + jnp.sum(jnp.exp(scores - new_top[..., None]), axis=-1)
        return ((new_top, mass), None)

    (top, mass), _ = lax.scan(absorb, (top, mass), (window_keys, window_pos, window_member))
    log_total = top + jnp.log(mass)

    def attend_part(key_block, value_block, key_pos, key_member):
        scores = scores_for(key_block, key_pos, key_member)
        probs_low = jnp.exp(scores - log_total[..., None]).astype(jnp.bfloat16)
        return jnp.einsum(
            "agqk,kad->agqd", probs_low, value_block, preferred_element_type=jnp.float32
        )

    def attend_step(total, inputs):
        return (total + attend_part(*inputs), None)

    attended = attend_part(keys, own_values, own_pos, own_member)
    attended, _ = lax.scan(
        attend_step, attended, (window_keys, window_values, window_pos, window_member)
    )
    grad_heads = grad_out.reshape(rows, kv_here, group, HEAD_DIM)
    delta = jnp.einsum("qagd,agqd->agq", grad_heads.astype(jnp.float32), attended)

    def differentiate(key_block, value_block, key_pos, key_member):
        scores = scores_for(key_block, key_pos, key_member)
        probs = jnp.exp(scores - log_total[..., None])
        probs_low = probs.astype(jnp.bfloat16)
        grad_values = jnp.einsum(
            "agqk,qagd->kad", probs_low, grad_heads, preferred_element_type=jnp.float32
        )
        grad_probs = jnp.einsum(
            "qagd,kad->agqk", grad_heads, value_block, preferred_element_type=jnp.float32
        )
        grad_scores = (probs * (grad_probs - delta[..., None])).astype(jnp.bfloat16)
        grad_query = (
            jnp.einsum("agqk,kad->qagd", grad_scores, key_block, preferred_element_type=jnp.float32)
            * scale
        )
        grad_keys = (
            jnp.einsum("agqk,qagd->kad", grad_scores, query, preferred_element_type=jnp.float32)
            * scale
        )
        return (grad_query, grad_keys, grad_values)

    query_grad, own_key_grad, own_value_grad = differentiate(keys, own_values, own_pos, own_member)

    def visit(total, inputs):
        grad_query, grad_keys, grad_values = differentiate(*inputs)
        return (total + grad_query, (grad_keys, grad_values))

    query_grad, (far_keys, far_values) = lax.scan(
        visit, query_grad, (window_keys, window_values, window_pos, window_member)
    )
    far_keys = far_keys.reshape(span, rows, kv_cols)
    far_values = far_values.reshape(span, rows, kv_cols)
    levels = (span - 1).bit_length()
    extra = 2**levels - span
    filler = jnp.zeros((extra, rows, kv_cols), jnp.float32)
    stack = (
        jnp.concatenate([far_keys[::-1], filler], axis=0),
        jnp.concatenate([far_values[::-1], filler], axis=0),
    )
    hops = [2**level for level in reversed(range(levels))] + [1]
    for number, hop in enumerate(hops):
        if number < levels:
            moving = (stack[0][hop:], stack[1][hop:])
        else:
            moving = stack
        arrived = (
            shifted(moving[0].astype(jnp.bfloat16), "seq", -hop).astype(jnp.float32),
            shifted(moving[1].astype(jnp.bfloat16), "seq", -hop).astype(jnp.float32),
        )
        if number < levels:
            stack = (stack[0][:hop] + arrived[0], stack[1][:hop] + arrived[1])
        else:
            stack = arrived
    returned = (stack[0][0], stack[1][0])
    key_grad = own_key_grad.reshape(rows, kv_cols) + returned[0]
    value_grad = own_value_grad.reshape(rows, kv_cols) + returned[1]
    grad_query = (
        rotate(query_grad.reshape(rows, heads_here, HEAD_DIM), cosine, sine, -1.0)
        .astype(jnp.bfloat16)
        .reshape(rows, head_cols)
    )
    grad_key = (
        rotate(key_grad.reshape(rows, kv_here, HEAD_DIM), cosine, sine, -1.0)
        .astype(jnp.bfloat16)
        .reshape(rows, kv_cols)
    )
    grad_value = value_grad.astype(jnp.bfloat16)
    grad_all = jnp.concatenate([grad_query, grad_key, grad_value], axis=1)
    term = lax.dot_general(grad_all, panel, CONTRACT_LAST, preferred_element_type=jnp.float32)
    grad_tokens = summed_on_arrival(term.astype(jnp.bfloat16), "mp", 1).astype(jnp.bfloat16)
    grad_weights = lax.psum_scatter(
        lax.dot_general(whole, grad_all, CONTRACT_FIRST, preferred_element_type=jnp.float32).astype(
            jnp.bfloat16
        ),
        "seq",
        scatter_dimension=0,
        tiled=True,
    ).astype(jnp.float32)
    return (
        grad_tokens,
        grad_weights[:, :head_cols],
        grad_weights[:, head_cols : head_cols + kv_cols],
        grad_weights[:, head_cols + kv_cols :],
    )


def solution(mesh):
    placed = (P("seq", "mp"), P("seq", "mp"), P("seq", "mp"), P("seq", "mp"), P("seq", "mp"), P())
    return jax.shard_map(
        local,
        mesh=mesh,
        in_specs=placed,
        out_specs=(P("seq", "mp"), P("seq", "mp"), P("seq", "mp"), P("seq", "mp")),
        check_vma=False,
    )
```

profile of v0, /device:TPU:2, one launch (start us, length us, event | category | flops | bytes accessed | tf_op | source)
XLA Modules:
  0.0 652.3 jit_solution(11152818374100308907)
XLA Ops:
  11.5 6.0 all-to-all-start
  22.0 21.4 %all-to-all-done = bf16[8,256,512]{1,2,0:T(8,128)(2,1)S(1)} async-done(((bf16[8,256,512]{1,2,0:T(8,128)(2,1)}), bf16[8,256,512]{1,2,0:T(8,128)(2,1)S(1)}, u32[]{:S(2)}, u32[]{:S(2)}) %all-to-all-start) | async-done | bytes 2097184 | tf_op jit(solution)/shard_map/all_to_all | solution.py:16
  43.3 76.7 %all-gather.2.cloned.1.call-done = bf16[4096,768]{1,0:T(8,128)(2,1)} async-done(((bf16[128,768]{1,0:T(8,128)(2,1)}), bf16[4096,768]{1,0:T(8,128)(2,1)}) %all-gather.2.cloned.1.call-update) | async-done | bytes 6291472 | tf_op jit(solution)/shard_map/all_gather | solution.py:89
  120.1 4.6 convolution_bitcast_fusion.4
  128.1 3.7 collective-permute-start.5
  135.8 3.7 collective-permute-start.6
  149.8 3.6 collective-permute-start.3
  156.1 4.2 collective-permute-start.8
  160.4 5.0 collective-permute-done.3
  167.9 7.8 %collective-permute-start.4 = (bf16[8,256,128]{1,2,0:T(8,128)(2,1)}, bf16[8,256,128]{1,2,0:T(8,128)(2,1)}, u32[]{:S(2)}, u32[]{:S(2)}) collective-permute-start(bf16[8,256,128]{1,2,0:T(8,128)(2,1)} %pad_maximum_fusion), channel_id=1, source_target_pairs={{0,64},{8,72},{16,80},{24,88},{32,96},{40,104},{48,112},{56,120},{... | collective-permute-start | bytes 1572872 | tf_op jit(solution)/shard_map/ppermute | solution.py:35
  181.3 17.1 %collective-permute-start.9 = (bf16[8,256,128]{1,2,0:T(8,128)(2,1)}, bf16[8,256,128]{1,2,0:T(8,128)(2,1)}, u32[]{:S(2)}, u32[]{:S(2)}) collective-permute-start(bf16[8,256,128]{1,2,0:T(8,128)(2,1)} %pad_maximum_fusion.1), channel_id=1, source_target_pairs={{0,64},{8,72},{16,80},{24,88},{32,96},{40,104},{48,112},{56,120},{... | collective-permute-start | bytes 1572872 | tf_op jit(solution)/shard_map/ppermute | solution.py:35
  206.1 14.3 %collective-permute-done.9 = bf16[8,256,128]{1,2,0:T(8,128)(2,1)} collective-permute-done((bf16[8,256,128]{1,2,0:T(8,128)(2,1)}, bf16[8,256,128]{1,2,0:T(8,128)(2,1)}, u32[]{:S(2)}, u32[]{:S(2)}) %collective-permute-start.9) | collective-permute-done | bytes 524320 | tf_op jit(solution)/shard_map/ppermute | solution.py:35
  229.8 29.3 %while.39 = (s32[]{:T(128)}, f32[1,4,256]{2,1,0:T(4,128)S(1)}, f32[1,4,256]{2,1,0:T(4,128)S(1)}, s32[8,512]{1,0:T(8,128)}, s32[256]{0:T(256)S(1)}, /*index=5*/s3...) while((s32[]{:T(128)}, f32[1,4,256]{2,1,0:T(4,128)S(1)}, ...), condition=%wide.region_9.10_spmd.clone, body=%wide.region_6.9_spmd.clone.sunk | while | flops 138808064 | bytes 5050493 | solution.py:149
  260.3 37.7 %while.40 = (s32[]{:T(128)}, f32[1,4,256,128]{3,2,1,0:T(8,128)}, s32[8,512]{1,0:T(8,128)}, s32[256]{0:T(256)S(1)}, s32[8,512]{1,0:T(8,128)}, /*index=5*/bf16[8,5...) while((s32[]{:T(128)}, f32[1,4,256,128]{3,2,1,0:T(8,128)}, ...), condition=%wide.region_11.12_spmd.clone, body=%wide.region_10.11_spmd.clone.sunk | while | flops 271581952 | bytes 1856641 | solution.py:163
  302.8 65.6 %while.41 = (s32[]{:T(128)}, f32[256,1,4,128]{0,3,2,1:T(8,128)S(1)}, f32[8,512,1,128]{3,1,2,0:T(8,128)}, f32[8,512,1,128]{3,1,2,0:T(8,128)}, bf16[8,512,1,128]{3...) while((s32[]{:T(128)}, ...), condition=%wide.region_13.14_spmd.clone, body=%wide.region_12.13_spmd.clone.sunk | while | flops 676004608 | bytes 12738741 | solution.py:196
  402.3 18.1 %collective-permute-done.11 = bf16[4,256,128]{1,2,0:T(8,128)(2,1)S(1)} collective-permute-done((bf16[4,256,128]{1,2,0:T(8,128)(2,1)S(1)}, bf16[4,256,128]{1,2,0:T(8,128)(2,1)S(1)}, u32[]{:S(2)}, u32[]{:S(2)}) %collective-permute-start.11) | collective-permute-done | bytes 262176 | tf_op jit(solution)/shard_map/ppermute | solution.py:35
  421.9 12.4 %collective-permute-done.16 = bf16[4,256,128]{1,2,0:T(8,128)(2,1)S(1)} collective-permute-done((bf16[4,256,128]{1,2,0:T(8,128)(2,1)S(1)}, bf16[4,256,128]{1,2,0:T(8,128)(2,1)S(1)}, u32[]{:S(2)}, u32[]{:S(2)}) %collective-permute-start.16) | collective-permute-done | bytes 262176 | tf_op jit(solution)/shard_map/ppermute | solution.py:35
  435.8 25.6 %collective-permute-done.12 = bf16[2,256,128]{1,2,0:T(8,128)(2,1)S(1)} collective-permute-done((bf16[2,256,128]{1,2,0:T(8,128)(2,1)S(1)}, bf16[2,256,128]{1,2,0:T(8,128)(2,1)S(1)}, u32[]{:S(2)}, u32[]{:S(2)}) %collective-permute-start.12) | collective-permute-done | bytes 131104 | tf_op jit(solution)/shard_map/ppermute | solution.py:35
  462.8 6.2 collective-permute-done.17
  477.7 4.4 fusion.68
  482.2 8.6 %copy.196 = bf16[4096,768]{1,0:T(8,128)(2,1)} copy(bf16[4096,768]{0,1:T(8,128)(2,1)} %fusion.68) | data formatting | bytes 12582912
  490.8 4.6 convolution_convert_fusion.1
  495.7 30.4 %all_to_all.10 = bf16[8,256,512]{2,1,0:T(8,128)(2,1)S(1)} all-to-all(bf16[8,256,512]{2,1,0:T(8,128)(2,1)S(1)} %bitcast.388), channel_id=1, replica_groups=mesh['seq'=32,'mp'=8] {'mp'}, dimensions={0} | all-to-all | bytes 4194304 | tf_op jit(solution)/shard_map/all_to_all | solution.py:46
  527.1 114.9 %reduce-scatter.4.cloned.1.call-done = bf16[128,768]{1,0:T(8,128)(2,1)} async-done(((bf16[4096,768]{1,0:T(8,128)(2,1)}), bf16[128,768]{1,0:T(8,128)(2,1)}) %reduce-scatter.4.cloned.1.call-update) | async-done | bytes 196624
  (374 shorter events, 243.1 us)
Async XLA Ops:
  7.2 112.9 %all-gather.2.cloned.1.call-start = ((), (), s32[]{:S(2)}) async-start(), calls=%async_computation.3 | async-start | bytes 6488064 | tf_op jit(solution)/shard_map/all_gather | solution.py:89
  11.5 31.8 %all-to-all-start = ((bf16[8,256,512]{1,2,0:T(8,128)(2,1)}), bf16[8,256,512]{1,2,0:T(8,128)(2,1)S(1)}, u32[]{:S(2)}, u32[]{:S(2)}) async-start(bf16[8,256,512]{1,2,0:T(8,128)(2,1)} %broadcast_in_dim.60), calls=%async_computation | async-start | bytes 4194304 | tf_op jit(solution)/shard_map/all_to_all | solution.py:16
  17.5 624.5 %reduce-scatter.4.cloned.1.call-start = ((), (), s32[]{:S(2)}) async-start(), calls=%async_computation.4 | async-start | bytes 6488064
  43.3 81.4 %copy-start = (bf16[8,256,512]{1,2,0:T(8,128)(2,1)}, bf16[8,256,512]{1,2,0:T(8,128)(2,1)S(1)}, u32[]{:S(2)}) copy-start(bf16[8,256,512]{1,2,0:T(8,128)(2,1)S(1)} %all-to-all-done) | copy-start | bytes 6291460
  125.9 6.2 collective-permute-start
  128.1 7.7 %collective-permute-start.5 = (bf16[1,256,128]{1,2,0:T(8,128)(2,1)S(1)}, bf16[1,256,128]{1,2,0:T(8,128)(2,1)}, u32[]{:S(2)}, u32[]{:S(2)}) collective-permute-start(bf16[1,256,128]{1,2,0:T(8,128)(2,1)S(1)} %fusion.117), channel_id=1, source_target_pairs={{0,8},{8,16},{16,24},{24,32},{32,40},{40,48},{48,56},{56,64},{64,7... | collective-permute-start | bytes 196616 | tf_op jit(solution)/shard_map/ppermute | solution.py:35
  132.1 7.5 %collective-permute-start.1 = (bf16[1,256,128]{1,2,0:T(8,128)(2,1)S(1)}, bf16[1,256,128]{1,2,0:T(8,128)(2,1)S(1)}, u32[]{:S(2)}, u32[]{:S(2)}) collective-permute-start(bf16[1,256,128]{1,2,0:T(8,128)(2,1)S(1)} %collective-permute-done), channel_id=1, source_target_pairs={{0,8},{8,16},{16,24},{24,32},{32,40},{40,48},{48,56},{56,64},{64,7... | collective-permute-start | bytes 196616 | tf_op jit(solution)/shard_map/ppermute | solution.py:35
  135.8 9.5 %collective-permute-start.6 = (bf16[1,256,128]{1,2,0:T(8,128)(2,1)}, bf16[1,256,128]{1,2,0:T(8,128)(2,1)}, u32[]{:S(2)}, u32[]{:S(2)}) collective-permute-start(bf16[1,256,128]{1,2,0:T(8,128)(2,1)} %collective-permute-done.5), channel_id=1, source_target_pairs={{0,8},{8,16},{16,24},{24,32},{32,40},{40,48},{48,56},{56,64},{64,7... | collective-permute-start | bytes 196616 | tf_op jit(solution)/shard_map/ppermute | solution.py:35
  140.2 8.6 %collective-permute-start.2 = (bf16[2,256,128]{1,2,0:T(8,128)(2,1)}, bf16[2,256,128]{1,2,0:T(8,128)(2,1)}, u32[]{:S(2)}, u32[]{:S(2)}) collective-permute-start(bf16[2,256,128]{1,2,0:T(8,128)(2,1)} %pad_maximum_fusion.9), channel_id=1, source_target_pairs={{0,16},{8,24},{16,32},{24,40},{32,48},{40,56},{48,64},{56,72},{64,... | collective-permute-start | bytes 393224 | tf_op jit(solution)/shard_map/ppermute | solution.py:35
  146.2 7.6 %collective-permute-start.7 = (bf16[2,256,128]{1,2,0:T(8,128)(2,1)S(1)}, bf16[2,256,128]{1,2,0:T(8,128)(2,1)S(1)}, u32[]{:S(2)}, u32[]{:S(2)}) collective-permute-start(bf16[2,256,128]{1,2,0:T(8,128)(2,1)S(1)} %pad_maximum_fusion.10), channel_id=1, source_target_pairs={{0,16},{8,24},{16,32},{24,40},{32,48},{40,56},{48,64},{56,72},{64,... | collective-permute-start | bytes 393224 | tf_op jit(solution)/shard_map/ppermute | solution.py:35
  149.8 15.6 %collective-permute-start.3 = (bf16[4,256,128]{1,2,0:T(8,128)(2,1)S(1)}, bf16[4,256,128]{1,2,0:T(8,128)(2,1)S(1)}, u32[]{:S(2)}, u32[]{:S(2)}) collective-permute-start(bf16[4,256,128]{1,2,0:T(8,128)(2,1)S(1)} %pad_maximum_fusion.3), channel_id=1, source_target_pairs={{0,32},{8,40},{16,48},{24,56},{32,64},{40,72},{48,80},{56,88},{64,... | collective-permute-start | bytes 786440 | tf_op jit(solution)/shard_map/ppermute | solution.py:35
  156.1 23.2 %collective-permute-start.8 = (bf16[4,256,128]{1,2,0:T(8,128)(2,1)}, bf16[4,256,128]{1,2,0:T(8,128)(2,1)}, u32[]{:S(2)}, u32[]{:S(2)}) collective-permute-start(bf16[4,256,128]{1,2,0:T(8,128)(2,1)} %pad_maximum_fusion.4), channel_id=1, source_target_pairs={{0,32},{8,40},{16,48},{24,56},{32,64},{40,72},{48,80},{56,88},{64,... | collective-permute-start | bytes 786440 | tf_op jit(solution)/shard_map/ppermute | solution.py:35
  167.9 30.5 %collective-permute-start.4 = (bf16[8,256,128]{1,2,0:T(8,128)(2,1)}, bf16[8,256,128]{1,2,0:T(8,128)(2,1)}, u32[]{:S(2)}, u32[]{:S(2)}) collective-permute-start(bf16[8,256,128]{1,2,0:T(8,128)(2,1)} %pad_maximum_fusion), channel_id=1, source_target_pairs={{0,64},{8,72},{16,80},{24,88},{32,96},{40,104},{48,112},{56,120},{... | collective-permute-start | bytes 1572872 | tf_op jit(solution)/shard_map/ppermute | solution.py:35
  181.3 39.1 %collective-permute-start.9 = (bf16[8,256,128]{1,2,0:T(8,128)(2,1)}, bf16[8,256,128]{1,2,0:T(8,128)(2,1)}, u32[]{:S(2)}, u32[]{:S(2)}) collective-permute-start(bf16[8,256,128]{1,2,0:T(8,128)(2,1)} %pad_maximum_fusion.1), channel_id=1, source_target_pairs={{0,64},{8,72},{16,80},{24,88},{32,96},{40,104},{48,112},{56,120},{... | collective-permute-start | bytes 1572872 | tf_op jit(solution)/shard_map/ppermute | solution.py:35
  372.6 21.2 %collective-permute-start.10 = (bf16[8,256,128]{1,2,0:T(8,128)(2,1)}, bf16[8,256,128]{1,2,0:T(8,128)(2,1)}, u32[]{:S(2)}, u32[]{:S(2)}) collective-permute-start(bf16[8,256,128]{1,2,0:T(8,128)(2,1)} %slice.232), channel_id=1, source_target_pairs={{64,0},{72,8},{80,16},{88,24},{96,32},{104,40},{112,48},{120,56},{... | collective-permute-start | bytes 1572872 | tf_op jit(solution)/shard_map/ppermute | solution.py:35
  380.0 19.3 %collective-permute-start.15 = (bf16[8,256,128]{1,2,0:T(8,128)(2,1)}, bf16[8,256,128]{1,2,0:T(8,128)(2,1)}, u32[]{:S(2)}, u32[]{:S(2)}) collective-permute-start(bf16[8,256,128]{1,2,0:T(8,128)(2,1)} %slice.231), channel_id=1, source_target_pairs={{64,0},{72,8},{80,16},{88,24},{96,32},{104,40},{112,48},{120,56},{... | collective-permute-start | bytes 1572872 | tf_op jit(solution)/shard_map/ppermute | solution.py:35
  395.3 25.1 %collective-permute-start.11 = (bf16[4,256,128]{1,2,0:T(8,128)(2,1)S(1)}, bf16[4,256,128]{1,2,0:T(8,128)(2,1)S(1)}, u32[]{:S(2)}, u32[]{:S(2)}) collective-permute-start(bf16[4,256,128]{1,2,0:T(8,128)(2,1)S(1)} %slice.234), channel_id=1, source_target_pairs={{32,0},{40,8},{48,16},{56,24},{64,32},{72,40},{80,48},{88,56},{96,... | collective-permute-start | bytes 786440 | tf_op jit(solution)/shard_map/ppermute | solution.py:35
  400.6 33.8 %collective-permute-start.16 = (bf16[4,256,128]{1,2,0:T(8,128)(2,1)S(1)}, bf16[4,256,128]{1,2,0:T(8,128)(2,1)S(1)}, u32[]{:S(2)}, u32[]{:S(2)}) collective-permute-start(bf16[4,256,128]{1,2,0:T(8,128)(2,1)S(1)} %slice.233), channel_id=1, source_target_pairs={{32,0},{40,8},{48,16},{56,24},{64,32},{72,40},{80,48},{88,56},{96,... | collective-permute-start | bytes 786440 | tf_op jit(solution)/shard_map/ppermute | solution.py:35
  420.5 41.0 %collective-permute-start.12 = (bf16[2,256,128]{1,2,0:T(8,128)(2,1)S(1)}, bf16[2,256,128]{1,2,0:T(8,128)(2,1)S(1)}, u32[]{:S(2)}, u32[]{:S(2)}) collective-permute-start(bf16[2,256,128]{1,2,0:T(8,128)(2,1)S(1)} %slice.236), channel_id=1, source_target_pairs={{16,0},{24,8},{32,16},{40,24},{48,32},{56,40},{64,48},{72,56},{80,... | collective-permute-start | bytes 393224 | tf_op jit(solution)/shard_map/ppermute | solution.py:35
  434.4 34.6 %collective-permute-start.17 = (bf16[2,256,128]{1,2,0:T(8,128)(2,1)S(1)}, bf16[2,256,128]{1,2,0:T(8,128)(2,1)S(1)}, u32[]{:S(2)}, u32[]{:S(2)}) collective-permute-start(bf16[2,256,128]{1,2,0:T(8,128)(2,1)S(1)} %slice.235), channel_id=1, source_target_pairs={{16,0},{24,8},{32,16},{40,24},{48,32},{56,40},{64,48},{72,56},{80,... | collective-permute-start | bytes 393224 | tf_op jit(solution)/shard_map/ppermute | solution.py:35
  461.5 8.9 %collective-permute-start.13 = (bf16[1,256,128]{1,2,0:T(8,128)(2,1)S(1)}, bf16[1,256,128]{1,2,0:T(8,128)(2,1)S(1)}, u32[]{:S(2)}, u32[]{:S(2)}) collective-permute-start(bf16[1,256,128]{1,2,0:T(8,128)(2,1)S(1)} %slice.238), channel_id=1, source_target_pairs={{8,0},{16,8},{24,16},{32,24},{40,32},{48,40},{56,48},{64,56},{72,6... | collective-permute-start | bytes 196616 | tf_op jit(solution)/shard_map/ppermute | solution.py:35
  469.1 3.1 collective-permute-start.18
  470.4 3.8 collective-permute-start.14
  472.2 5.5 collective-permute-start.19
  (26 other events, 320.0 us)
Sparse Core Ops, SparseCore 0:
  11.3 108.6 all-gather.1
  491.0 151.0 reduce-scatter.3
where the time goes:
time: 658 us; the launch traced here: 652 us
  waiting for transfers between devices  304 us (46%)
  matrix products  105 us (16%)
  local copies, waits for them, and re-layouts  75.4 us (11%)
  starting transfers between devices  69.7 us (11%)
  other arithmetic  52.3 us (8%)
  blocking collectives  30.4 us (5%)
  between operations  14.8 us (2%)
    unnamed x3, waiting for transfers between devices  115 us
    ppermute x20, waiting for transfers between devices, shifted(): return lax.ppermute(value, axis, pairs)  90.6 us
    all_gather x1, waiting for transfers between devices, local(): panel = lax.all_gather(weights_all, 'seq', axis=0, tiled=True)  76.7 us
    ppermute x20, starting transfers between devices, shifted(): return lax.ppermute(value, axis, pairs)  63.7 us
    all_to_all x1, blocking collectives, summed_on_arrival(): parts = lax.all_to_all(split_up(value, dim, peers), axis, 0, 0, tiled=True)  30.4 us
    unnamed x70, local copies, waits for them, and re-layouts  26.1 us
    dot_general x9, matrix products, attend_part(): jnp.einsum('agqk,kad->agqd', probs_low, value_block, preferred_element_ty...  24.9 us
    dot_general x17, matrix products, scores_for(): jnp.einsum('qagd,kad->agqk', query, key_block, preferred_element_type=jnp...  23.5 us
  transfers between devices with their start and end apart: 23, of which 14 were waited for; matrix products, arithmetic and copies ran while one was open for 9% of the time, Pallas kernels for 0%

commit v1 on v0

--- a/solution.py
+++ b/solution.py
@@ -9,6 +9,13 @@
 THETA = 10000.0
 CONTRACT_LAST = (((1,), (1,)), ((), ()))
 CONTRACT_FIRST = (((0,), (0,)), ((), ()))
+
+
+def gather_over(block, axis, d):
+    n_dev = lax.axis_size(axis)
+    blocks = jnp.stack([block for _ in range(n_dev)])
+    blocks = lax.all_to_all(blocks, axis, split_axis=0, concat_axis=0)
+    return jnp.concatenate(blocks, axis=d)
 
 
 def from_everyone(value, axis):
@@ -86,7 +93,7 @@
     cosine, sine = rope_tables(own_offset)
     weights_all = jnp.concatenate([w_query, w_key, w_value], axis=1)
     whole = gather_directly(tokens, "mp", 1)
-    panel = lax.all_gather(weights_all, "seq", axis=0, tiled=True)
+    panel = gather_over(weights_all, "seq", 0)
     projected = jnp.dot(whole, panel, preferred_element_type=jnp.float32)
     query = rotate(projected[:, :head_cols].reshape(rows, heads_here, HEAD_DIM), cosine, sine, 1.0)
     query = query.astype(jnp.bfloat16).reshape(rows, kv_here, group, HEAD_DIM)

time: 658 us -> 717 us (1.090)
  waiting for transfers between devices: 304 us -> 344 us
  starting transfers between devices: 69.7 us -> 82.6 us
    all_to_all x0 -> x1, waiting for transfers between devices: none -> 138 us  [gather_over(): blocks = lax.all_to_all(blocks, axis, split_axis=0, concat_axis=0)]
    all_gather x1 -> x0, waiting for transfers between devices: 76.7 us -> none  [local(): panel = lax.all_gather(weights_all, 'seq', axis=0, tiled=True)]
    ppermute x20, waiting for transfers between devices: 90.6 us -> 69.2 us  [shifted(): return lax.ppermute(value, axis, pairs)]
    all_to_all x0 -> x1, starting transfers between devices: none -> 11.4 us  [gather_over(): blocks = lax.all_to_all(blocks, axis, split_axis=0, concat_axis=0)]
    unnamed x3 -> x2, waiting for transfers between devices: 115 us -> 111 us
    unnamed x70 -> x76, local copies, waits for them, and re-layouts: 26.1 us -> 26.2 us
  transfers between devices with their start and end apart: 23 -> 23, of which waited for: 14 -> 14; matrix products, arithmetic and copies ran while one was open for 9% -> 8% of each run, Pallas kernels for 0% -> 0%
where the time goes in v1:
time: 717 us; the launch traced here: 712 us
  waiting for transfers between devices  344 us (48%)
  matrix products  106 us (15%)
  starting transfers between devices  82.6 us (12%)
  local copies, waits for them, and re-layouts  78.8 us (11%)
  other arithmetic  50.7 us (7%)
  blocking collectives  34.2 us (5%)
  between operations  14.9 us (2%)
    all_to_all x1, waiting for transfers between devices, gather_over(): blocks = lax.all_to_all(blocks, axis, split_axis=0, concat_axis=0)  138 us
    unnamed x2, waiting for transfers between devices  111 us
    ppermute x20, waiting for transfers between devices, shifted(): return lax.ppermute(value, axis, pairs)  69.2 us
    ppermute x20, starting transfers between devices, shifted(): return lax.ppermute(value, axis, pairs)  65.2 us
    all_to_all x1, blocking collectives, summed_on_arrival(): parts = lax.all_to_all(split_up(value, dim, peers), axis, 0, 0, tiled=True)  34.2 us
    unnamed x76, local copies, waits for them, and re-layouts  26.2 us
    all_to_all x1, waiting for transfers between devices, from_everyone(): lax.all_to_all(jnp.broadcast_to(value[None], (peers, *value.shape)), axis...  25.7 us
    dot_general x9, matrix products, attend_part(): jnp.einsum('agqk,kad->agqd', probs_low, value_block, preferred_element_ty...  25.5 us
  transfers between devices with their start and end apart: 23, of which 14 were waited for; matrix products, arithmetic and copies ran while one was open for 8% of the time, Pallas kernels for 0%

profile of v1, /device:TPU:2, one launch (start us, length us, event | category | flops | bytes accessed | tf_op | source)
XLA Modules:
  0.0 711.8 jit_solution(14812257508585160456)
XLA Ops:
  9.7 6.0 all-to-all-start.1
  15.8 25.7 %all-to-all-done.1 = bf16[8,256,512]{1,2,0:T(8,128)(2,1)S(1)} async-done(((bf16[8,256,512]{1,2,0:T(8,128)(2,1)}), bf16[8,256,512]{1,2,0:T(8,128)(2,1)S(1)}, u32[]{:S(2)}, u32[]{:S(2)}) %all-to-all-start.1) | async-done | bytes 2097184 | tf_op jit(solution)/shard_map/all_to_all | solution.py:23
  44.8 11.4 %all-to-all-start = ((bf16[32,128,768]{2,1,0:T(8,128)(2,1)}), bf16[32,128,768]{2,1,0:T(8,128)(2,1)}, u32[]{:S(2)}, u32[]{:S(2)}) async-start(bf16[32,128,768]{2,1,0:T(8,128)(2,1)} %stack.2), calls=%async_computation | async-start | bytes 12582912 | tf_op jit(solution)/shard_map/all_to_all | solution.py:17
  60.8 137.8 %all-to-all-done = bf16[32,128,768]{2,1,0:T(8,128)(2,1)} async-done(((bf16[32,128,768]{2,1,0:T(8,128)(2,1)}), bf16[32,128,768]{2,1,0:T(8,128)(2,1)}, u32[]{:S(2)}, u32[]{:S(2)}) %all-to-all-start) | async-done | bytes 6291488 | tf_op jit(solution)/shard_map/all_to_all | solution.py:17
  198.7 4.6 convolution_bitcast_fusion.4
  211.9 4.0 collective-permute-start.6
  216.5 6.5 collective-permute-start.2
  234.5 4.1 collective-permute-start.8
  238.6 4.3 collective-permute-done.3
  245.4 15.7 %collective-permute-start.4 = (bf16[8,256,128]{1,2,0:T(8,128)(2,1)}, bf16[8,256,128]{1,2,0:T(8,128)(2,1)}, u32[]{:S(2)}, u32[]{:S(2)}) collective-permute-start(bf16[8,256,128]{1,2,0:T(8,128)(2,1)} %pad_maximum_fusion), channel_id=1, source_target_pairs={{0,64},{8,72},{16,80},{24,88},{32,96},{40,104},{48,112},{56,120},{... | collective-permute-start | bytes 1572872 | tf_op jit(solution)/shard_map/ppermute | solution.py:42
  266.7 11.0 %collective-permute-start.9 = (bf16[8,256,128]{1,2,0:T(8,128)(2,1)}, bf16[8,256,128]{1,2,0:T(8,128)(2,1)}, u32[]{:S(2)}, u32[]{:S(2)}) collective-permute-start(bf16[8,256,128]{1,2,0:T(8,128)(2,1)} %pad_maximum_fusion.1), channel_id=1, source_target_pairs={{0,64},{8,72},{16,80},{24,88},{32,96},{40,104},{48,112},{56,120},{... | collective-permute-start | bytes 1572872 | tf_op jit(solution)/shard_map/ppermute | solution.py:42
  286.0 13.4 %collective-permute-done.9 = bf16[8,256,128]{1,2,0:T(8,128)(2,1)} collective-permute-done((bf16[8,256,128]{1,2,0:T(8,128)(2,1)}, bf16[8,256,128]{1,2,0:T(8,128)(2,1)}, u32[]{:S(2)}, u32[]{:S(2)}) %collective-permute-start.9) | collective-permute-done | bytes 524320 | tf_op jit(solution)/shard_map/ppermute | solution.py:42
  308.9 29.3 %while.39 = (s32[]{:T(128)}, f32[1,4,256]{2,1,0:T(4,128)S(1)}, f32[1,4,256]{2,1,0:T(4,128)S(1)}, s32[8,512]{1,0:T(8,128)}, s32[256]{0:T(256)S(1)}, /*index=5*/s3...) while((s32[]{:T(128)}, f32[1,4,256]{2,1,0:T(4,128)S(1)}, ...), condition=%wide.region_9.10_spmd.clone, body=%wide.region_6.9_spmd.clone.sunk | while | flops 138808064 | bytes 5050493 | solution.py:156
  339.5 38.3 %while.40 = (s32[]{:T(128)}, f32[1,4,256,128]{3,2,1,0:T(8,128)}, s32[8,512]{1,0:T(8,128)}, s32[256]{0:T(256)S(1)}, s32[8,512]{1,0:T(8,128)}, /*index=5*/bf16[8,5...) while((s32[]{:T(128)}, f32[1,4,256,128]{3,2,1,0:T(8,128)}, ...), condition=%wide.region_11.12_spmd.clone, body=%wide.region_10.11_spmd.clone.sunk | while | flops 271581952 | bytes 1856641 | solution.py:170
  382.6 65.6 %while.41 = (s32[]{:T(128)}, f32[256,1,4,128]{0,3,2,1:T(8,128)S(1)}, f32[8,512,1,128]{3,1,2,0:T(8,128)}, f32[8,512,1,128]{3,1,2,0:T(8,128)}, bf16[8,512,1,128]{3...) while((s32[]{:T(128)}, ...), condition=%wide.region_13.14_spmd.clone, body=%wide.region_12.13_spmd.clone.sunk | while | flops 676004608 | bytes 12738741 | solution.py:203
  471.2 4.7 collective-permute-done.10
  485.5 26.4 %collective-permute-done.11 = bf16[4,256,128]{1,2,0:T(8,128)(2,1)S(1)} collective-permute-done((bf16[4,256,128]{1,2,0:T(8,128)(2,1)S(1)}, bf16[4,256,128]{1,2,0:T(8,128)(2,1)S(1)}, u32[]{:S(2)}, u32[]{:S(2)}) %collective-permute-start.11) | collective-permute-done | bytes 262176 | tf_op jit(solution)/shard_map/ppermute | solution.py:42
  513.4 8.9 %collective-permute-done.16 = bf16[4,256,128]{1,2,0:T(8,128)(2,1)S(1)} collective-permute-done((bf16[4,256,128]{1,2,0:T(8,128)(2,1)S(1)}, bf16[4,256,128]{1,2,0:T(8,128)(2,1)S(1)}, u32[]{:S(2)}, u32[]{:S(2)}) %collective-permute-start.16) | collective-permute-done | bytes 262176 | tf_op jit(solution)/shard_map/ppermute | solution.py:42
  525.2 4.2 collective-permute-done.17
  537.2 4.4 fusion.68
  541.6 8.6 %copy.196 = bf16[4096,768]{1,0:T(8,128)(2,1)} copy(bf16[4096,768]{0,1:T(8,128)(2,1)} %fusion.68) | data formatting | bytes 12582912
  550.3 4.6 convolution_convert_fusion.1
  555.1 34.2 %all_to_all.15 = bf16[8,256,512]{2,1,0:T(8,128)(2,1)S(1)} all-to-all(bf16[8,256,512]{2,1,0:T(8,128)(2,1)S(1)} %bitcast.389), channel_id=1, replica_groups=mesh['seq'=32,'mp'=8] {'mp'}, dimensions={0} | all-to-all | bytes 4194304 | tf_op jit(solution)/shard_map/all_to_all | solution.py:53
  590.4 111.1 %reduce-scatter.4.cloned.1.call-done = bf16[128,768]{1,0:T(8,128)(2,1)} async-done(((bf16[4096,768]{1,0:T(8,128)(2,1)}), bf16[128,768]{1,0:T(8,128)(2,1)}) %reduce-scatter.4.cloned.1.call-update) | async-done | bytes 196624
  (380 shorter events, 244.4 us)
Async XLA Ops:
  9.7 31.7 %all-to-all-start.1 = ((bf16[8,256,512]{1,2,0:T(8,128)(2,1)}), bf16[8,256,512]{1,2,0:T(8,128)(2,1)S(1)}, u32[]{:S(2)}, u32[]{:S(2)}) async-start(bf16[8,256,512]{1,2,0:T(8,128)(2,1)} %broadcast_in_dim.60), calls=%async_computation.1 | async-start | bytes 4194304 | tf_op jit(solution)/shard_map/all_to_all | solution.py:23
  41.5 157.2 %copy-start = (bf16[8,256,512]{1,2,0:T(8,128)(2,1)}, bf16[8,256,512]{1,2,0:T(8,128)(2,1)S(1)}, u32[]{:S(2)}) copy-start(bf16[8,256,512]{1,2,0:T(8,128)(2,1)S(1)} %all-to-all-done.1) | copy-start | bytes 6291460
  44.8 153.8 %all-to-all-start = ((bf16[32,128,768]{2,1,0:T(8,128)(2,1)}), bf16[32,128,768]{2,1,0:T(8,128)(2,1)}, u32[]{:S(2)}, u32[]{:S(2)}) async-start(bf16[32,128,768]{2,1,0:T(8,128)(2,1)} %stack.2), calls=%async_computation | async-start | bytes 12582912 | tf_op jit(solution)/shard_map/all_to_all | solution.py:17
  56.3 645.2 %reduce-scatter.4.cloned.1.call-start = ((), (), s32[]{:S(2)}) async-start(), calls=%async_computation.4 | async-start | bytes 6488064
  204.5 3.9 collective-permute-start
  205.8 6.0 collective-permute-start.5
  208.4 7.4 %collective-permute-start.1 = (bf16[1,256,128]{1,2,0:T(8,128)(2,1)S(1)}, bf16[1,256,128]{1,2,0:T(8,128)(2,1)S(1)}, u32[]{:S(2)}, u32[]{:S(2)}) collective-permute-start(bf16[1,256,128]{1,2,0:T(8,128)(2,1)S(1)} %collective-permute-done), channel_id=1, source_target_pairs={{0,8},{8,16},{16,24},{24,32},{32,40},{40,48},{48,56},{56,64},{64,7... | collective-permute-start | bytes 196616 | tf_op jit(solution)/shard_map/ppermute | solution.py:42
  211.9 12.7 %collective-permute-start.6 = (bf16[1,256,128]{1,2,0:T(8,128)(2,1)}, bf16[1,256,128]{1,2,0:T(8,128)(2,1)}, u32[]{:S(2)}, u32[]{:S(2)}) collective-permute-start(bf16[1,256,128]{1,2,0:T(8,128)(2,1)} %collective-permute-done.5), channel_id=1, source_target_pairs={{0,8},{8,16},{16,24},{24,32},{32,40},{40,48},{48,56},{56,64},{64,7... | collective-permute-start | bytes 196616 | tf_op jit(solution)/shard_map/ppermute | solution.py:42
  216.5 11.6 %collective-permute-start.2 = (bf16[2,256,128]{1,2,0:T(8,128)(2,1)}, bf16[2,256,128]{1,2,0:T(8,128)(2,1)}, u32[]{:S(2)}, u32[]{:S(2)}) collective-permute-start(bf16[2,256,128]{1,2,0:T(8,128)(2,1)} %pad_maximum_fusion.9), channel_id=1, source_target_pairs={{0,16},{8,24},{16,32},{24,40},{32,48},{40,56},{48,64},{56,72},{64,... | collective-permute-start | bytes 393224 | tf_op jit(solution)/shard_map/ppermute | solution.py:42
  225.5 6.8 collective-permute-start.7
  229.2 13.8 %collective-permute-start.3 = (bf16[4,256,128]{1,2,0:T(8,128)(2,1)S(1)}, bf16[4,256,128]{1,2,0:T(8,128)(2,1)S(1)}, u32[]{:S(2)}, u32[]{:S(2)}) collective-permute-start(bf16[4,256,128]{1,2,0:T(8,128)(2,1)S(1)} %pad_maximum_fusion.3), channel_id=1, source_target_pairs={{0,32},{8,40},{16,48},{24,56},{32,64},{40,72},{48,80},{56,88},{64,... | collective-permute-start | bytes 786440 | tf_op jit(solution)/shard_map/ppermute | solution.py:42
  234.5 30.2 %collective-permute-start.8 = (bf16[4,256,128]{1,2,0:T(8,128)(2,1)}, bf16[4,256,128]{1,2,0:T(8,128)(2,1)}, u32[]{:S(2)}, u32[]{:S(2)}) collective-permute-start(bf16[4,256,128]{1,2,0:T(8,128)(2,1)} %pad_maximum_fusion.4), channel_id=1, source_target_pairs={{0,32},{8,40},{16,48},{24,56},{32,64},{40,72},{48,80},{56,88},{64,... | collective-permute-start | bytes 786440 | tf_op jit(solution)/shard_map/ppermute | solution.py:42
  245.4 32.9 %collective-permute-start.4 = (bf16[8,256,128]{1,2,0:T(8,128)(2,1)}, bf16[8,256,128]{1,2,0:T(8,128)(2,1)}, u32[]{:S(2)}, u32[]{:S(2)}) collective-permute-start(bf16[8,256,128]{1,2,0:T(8,128)(2,1)} %pad_maximum_fusion), channel_id=1, source_target_pairs={{0,64},{8,72},{16,80},{24,88},{32,96},{40,104},{48,112},{56,120},{... | collective-permute-start | bytes 1572872 | tf_op jit(solution)/shard_map/ppermute | solution.py:42
  266.7 32.6 %collective-permute-start.9 = (bf16[8,256,128]{1,2,0:T(8,128)(2,1)}, bf16[8,256,128]{1,2,0:T(8,128)(2,1)}, u32[]{:S(2)}, u32[]{:S(2)}) collective-permute-start(bf16[8,256,128]{1,2,0:T(8,128)(2,1)} %pad_maximum_fusion.1), channel_id=1, source_target_pairs={{0,64},{8,72},{16,80},{24,88},{32,96},{40,104},{48,112},{56,120},{... | collective-permute-start | bytes 1572872 | tf_op jit(solution)/shard_map/ppermute | solution.py:42
  452.4 23.5 %collective-permute-start.10 = (bf16[8,256,128]{1,2,0:T(8,128)(2,1)}, bf16[8,256,128]{1,2,0:T(8,128)(2,1)}, u32[]{:S(2)}, u32[]{:S(2)}) collective-permute-start(bf16[8,256,128]{1,2,0:T(8,128)(2,1)} %slice.232), channel_id=1, source_target_pairs={{64,0},{72,8},{80,16},{88,24},{96,32},{104,40},{112,48},{120,56},{... | collective-permute-start | bytes 1572872 | tf_op jit(solution)/shard_map/ppermute | solution.py:42
  459.8 22.8 %collective-permute-start.15 = (bf16[8,256,128]{1,2,0:T(8,128)(2,1)}, bf16[8,256,128]{1,2,0:T(8,128)(2,1)}, u32[]{:S(2)}, u32[]{:S(2)}) collective-permute-start(bf16[8,256,128]{1,2,0:T(8,128)(2,1)} %slice.231), channel_id=1, source_target_pairs={{64,0},{72,8},{80,16},{88,24},{96,32},{104,40},{112,48},{120,56},{... | collective-permute-start | bytes 1572872 | tf_op jit(solution)/shard_map/ppermute | solution.py:42
  477.5 34.4 %collective-permute-start.11 = (bf16[4,256,128]{1,2,0:T(8,128)(2,1)S(1)}, bf16[4,256,128]{1,2,0:T(8,128)(2,1)S(1)}, u32[]{:S(2)}, u32[]{:S(2)}) collective-permute-start(bf16[4,256,128]{1,2,0:T(8,128)(2,1)S(1)} %slice.234), channel_id=1, source_target_pairs={{32,0},{40,8},{48,16},{56,24},{64,32},{72,40},{80,48},{88,56},{96,... | collective-permute-start | bytes 786440 | tf_op jit(solution)/shard_map/ppermute | solution.py:42
  483.8 38.5 %collective-permute-start.16 = (bf16[4,256,128]{1,2,0:T(8,128)(2,1)S(1)}, bf16[4,256,128]{1,2,0:T(8,128)(2,1)S(1)}, u32[]{:S(2)}, u32[]{:S(2)}) collective-permute-start(bf16[4,256,128]{1,2,0:T(8,128)(2,1)S(1)} %slice.233), channel_id=1, source_target_pairs={{32,0},{40,8},{48,16},{56,24},{64,32},{72,40},{80,48},{88,56},{96,... | collective-permute-start | bytes 786440 | tf_op jit(solution)/shard_map/ppermute | solution.py:42
  512.0 11.8 %collective-permute-start.12 = (bf16[2,256,128]{1,2,0:T(8,128)(2,1)S(1)}, bf16[2,256,128]{1,2,0:T(8,128)(2,1)S(1)}, u32[]{:S(2)}, u32[]{:S(2)}) collective-permute-start(bf16[2,256,128]{1,2,0:T(8,128)(2,1)S(1)} %slice.236), channel_id=1, source_target_pairs={{16,0},{24,8},{32,16},{40,24},{48,32},{56,40},{64,48},{72,56},{80,... | collective-permute-start | bytes 393224 | tf_op jit(solution)/shard_map/ppermute | solution.py:42
  522.4 7.0 collective-permute-start.17
  523.9 6.8 collective-permute-start.13
  529.4 3.1 collective-permute-start.18
  530.7 3.8 collective-permute-start.14
  532.6 4.6 collective-permute-start.19
  (29 other events, 274.9 us)
Sparse Core Ops, SparseCore 0:
  550.4 151.0 reduce-scatter.3
